TPU v7x, 128 devices: a whole 4x4x4 slice. The times are simulated.
128 devices in a mesh: organ: 8 (over x, core), sub: 16 (over z, y).
Axes of the slice: x: 4, y: 4, z: 4, core: 2. Of those that a mesh axis runs over, the one named last changes fastest.
Arguments:
- dual_rhs: float32 [16, 8, 16, 5, 640], P(None, 'organ', 'sub')
- warm_start: float32 [16, 8, 16, 5, 640], P(None, 'organ', 'sub'), may hold values from -4 to 4
- inverse_blocks: float32 [8, 16, 5, 640, 640], P('organ', 'sub'), as said below
- coarse_basis: float32 [6, 8, 16, 5, 640], P(None, 'organ', 'sub')
- mortar_rows: float32 [8, 16, 512, 640], P('organ', 'sub'), may hold values from -0.25 to 0.25
- match_rounds: int32 [8, 16, 5], P('organ', 'sub'), may hold values from 0 to 4, each once within a row
- slave_owner: int32 [8, 16, 512, 1], P('organ', 'sub'), may hold values from 0 to 127; in each aligned block of 512 rows (0 to 511, 512 to 1023, ..., all dimensions but the last counted through in order) at most 8 rows name the same one
- slave_dofs: int32 [8, 16, 512], P('organ', 'sub'), may hold values from 0 to 639
- active_set: int32 [8, 16, 512], P('organ', 'sub'), may hold values 0 or 1
- row_counts: int32 [8, 16, 1], P('organ', 'sub'), may hold values from 384 to 512, as said below
Outputs:
- solution: float32 [16, 8, 16, 5, 640], P(None, 'organ', 'sub')
Inputs may be any that keep to these rules, and one draw needn't show every extreme that they name: `match_rounds`: each device's row lists every round's face once. `slave_owner`: in the rows of one device no owner is named more than 8 times; in some device one owner is named exactly 8 times. `row_counts`: some device has all 512 rows live. `inverse_blocks`: each face block is symmetric positive definite.
All inputs are finite; a program needn't handle non-finite values. No bound on the sum of `active_set` on one device may be relied on, other than what follows from the above.
Results may differ from a plain program's by a relative error of at most 0.0001.
Values sent between devices are 32-bit elements; how exact they have to be, the bound alone decides.
A program may use at most 128 MiB of HBM per device.

v0:
```python
import jax
import jax.numpy as jnp
from jax import lax
from jax.sharding import PartitionSpec as P

ITERS = 3
CAP = 8


def from_partner(value, axis, apart):
    mask = 2**apart
    pairs = [(source, source ^ mask) for source in range(lax.axis_size(axis))]
    return lax.ppermute(value, axis, pairs)


def local(
    dual_rhs,
    warm_start,
    inverse_blocks,
    coarse_basis,
    mortar_rows,
    match_rounds,
    slave_owner,
    slave_dofs,
    active_set,
    row_counts,
):
    directions = dual_rhs.shape[0]
    block_count = dual_rhs.shape[3]
    block_len = dual_rhs.shape[4]
    row_total = mortar_rows.shape[2]
    modes = coarse_basis.shape[0]
    right_side = dual_rhs.reshape(directions, block_count, block_len)
    starting = warm_start.reshape(directions, block_count, block_len)
    matrices = inverse_blocks.reshape(block_count, block_len, block_len)
    mode_basis = coarse_basis.reshape(modes, block_count, block_len)
    mortar = mortar_rows.reshape(row_total, block_len)
    rounds = match_rounds.reshape(-1)
    owner = slave_owner.reshape(-1)
    slave = slave_dofs.reshape(-1)
    live_rows = active_set.reshape(-1) * (
        jnp.arange(row_total, dtype=jnp.int32) < row_counts.reshape(())
    ).astype(jnp.int32)
    n_sub = lax.axis_size("sub")
    n_org = lax.axis_size("organ")
    devices = n_sub * n_org
    width = devices * CAP
    targets = (owner[:, None] == jnp.arange(devices, dtype=jnp.int32)[None, :]).astype(
        jnp.int32
    ) * live_rows[:, None]
    earlier = jnp.cumsum(targets, axis=0) - targets
    rank_row = jnp.sum(earlier * targets, axis=1)
    send_slot = jnp.where(live_rows > 0, owner * CAP + rank_row, width)
    outgoing_slave = jnp.full((width,), -1, jnp.int32).at[send_slot].set(slave, mode="drop")
    incoming_slave = lax.all_to_all(
        outgoing_slave, ("organ", "sub"), split_axis=0, concat_axis=0, tiled=True
    )
    incoming_ok = incoming_slave >= 0
    incoming_index = jnp.where(incoming_ok, incoming_slave, 0)

    def route(outgoing, backward):
        if backward:
            return lax.all_to_all(
                outgoing, ("organ", "sub"), split_axis=1, concat_axis=1, tiled=True
            )
        return lax.all_to_all(outgoing, ("organ", "sub"), split_axis=1, concat_axis=1, tiled=True)

    def contact_term(surface):
        row_vals = lax.dot_general(
            surface, mortar, (((1,), (1,)), ((), ())), precision=lax.Precision.HIGHEST
        )
        outgoing = (
            jnp.zeros((directions, width), jnp.float32).at[:, send_slot].set(row_vals, mode="drop")
        )
        received = route(outgoing, False)
        slave_vals = jnp.take(surface, incoming_index, axis=1)
        gap_vals = jnp.where(incoming_ok[None, :], received - slave_vals, 0.0)
        returned = route(gap_vals, True)
        row_gaps = jnp.take(returned, send_slot, axis=1, mode="fill", fill_value=0.0)
        master_part = jnp.dot(row_gaps, mortar, precision=lax.Precision.HIGHEST)
        slave_part = (
            jnp.zeros((directions, block_len), jnp.float32).at[:, incoming_index].add(gap_vals)
        )
        return master_part - slave_part

    block_ids = jnp.arange(block_count, dtype=jnp.int32)

    def jump(field):
        result = field
        for bit_index in range(3):
            selector = (rounds[bit_index] == block_ids).astype(jnp.float32)
            face_vals = lax.dynamic_index_in_dim(field, rounds[bit_index], 1, keepdims=False)
            remote = from_partner(face_vals, "sub", bit_index)
            result = result - selector[None, :, None] * remote[:, None, :]
        for bit_index in range(2):
            selector = (rounds[3 + bit_index] == block_ids).astype(jnp.float32)
            face_vals = lax.dynamic_index_in_dim(field, rounds[3 + bit_index], 1, keepdims=False)
            remote = from_partner(face_vals, "organ", bit_index)
            result = result - selector[None, :, None] * remote[:, None, :]
        return result.at[:, 0, :].add(contact_term(field[:, 0, :]))

    def operator(field):
        inner = jump(field)
        smoothed = jnp.einsum("kbn,bnm->kbm", inner, matrices, precision=lax.Precision.HIGHEST)
        return jump(smoothed)

    gram_local = jnp.einsum("mbn,lbn->ml", mode_basis, mode_basis, precision=lax.Precision.HIGHEST)
    gram_matrix = lax.psum(gram_local, "sub")
    factor = jnp.linalg.cholesky(gram_matrix)

    def project(resid):
        coeff_local = jnp.einsum("kbn,mbn->km", resid, mode_basis, precision=lax.Precision.HIGHEST)
        coeffs = lax.psum(coeff_local, "sub")
        solved = jax.scipy.linalg.cho_solve((factor, True), coeffs.T).T
        projected = resid - jnp.einsum(
            "km,mbn->kbn", solved, mode_basis, precision=lax.Precision.HIGHEST
        )
        rho_value = lax.psum(jnp.sum(resid * projected, axis=(1, 2)), ("organ", "sub"))
        return (projected, rho_value)

    solution = starting
    resid = right_side - operator(starting)
    projected, rho_now = project(resid)
    direction = projected
    for iteration in range(ITERS):
        image = operator(direction)
        curvature_sum = lax.psum(jnp.sum(direction * image, axis=(1, 2)), ("organ", "sub"))
        step_size = rho_now / curvature_sum
        solution = solution + step_size[:, None, None] * direction
        if iteration < ITERS - 1:
            resid = resid - step_size[:, None, None] * image
            projected, rho_new = project(resid)
            direction = projected + (rho_new / rho_now)[:, None, None] * direction
            rho_now = rho_new
    out_shape = (directions, 1, 1, block_count, block_len)
    return solution.reshape(out_shape)


def solution(mesh):
    in_specs = (
        P(None, "organ", "sub", None, None),
        P(None, "organ", "sub", None, None),
        P("organ", "sub", None, None, None),
        P(None, "organ", "sub", None, None),
        P("organ", "sub", None, None),
        P("organ", "sub", None),
        P("organ", "sub", None, None),
        P("organ", "sub", None),
        P("organ", "sub", None),
        P("organ", "sub", None),
    )
    out_specs = P(None, "organ", "sub", None, None)
    return jax.shard_map(local, mesh=mesh, in_specs=in_specs, out_specs=out_specs, check_vma=False)
```

profile of v0, /device:TPU:1, one launch (start us, length us, event | category | flops | bytes accessed | tf_op | source)
XLA Modules:
  0.0 895.5 jit_solution(13780328214375561958)
XLA Ops:
  6.5 11.5 %all-to-all-start = ((s32[128,8,1]{1,2,0:T(1,128)}), s32[128,8,1]{1,2,0:T(1,128)S(1)}, u32[]{:S(2)}, u32[]{:S(2)}) async-start(s32[128,8,1]{1,2,0:T(1,128)} %bitcast.20), calls=%async_computation | async-start | bytes 131072 | tf_op jit(solution)/shard_map/all_to_all | solution.py:55
  46.1 8.9 all-to-all-start.1
  96.0 7.3 all-to-all-start.3
  116.5 7.5 all-to-all-start.4
  136.9 33.9 %all-reduce.1 = (f32[6,16]{1,0:T(8,128)S(1)}, f32[6,6]{0,1:T(8,128)S(1)}) all-reduce(f32[6,16]{1,0:T(8,128)S(1)} %convolution_bitcast_fusion.5, f32[6,6]{0,1:T(8,128)S(1)} %copy-done.29), channel_id=1, replica_groups=mesh['organ'=8,'sub'=16] {'sub'}, use_global_device_ids=true, to_apply=%region_11.14 | all-reduce | flops 132 | bytes 1056 | tf_op jit(solution)/shard_map/psum | solution.py:113
  178.2 11.2 %all-to-all-start.5 = ((f32[128,1,128]{2,1,0:T(1,128)}), f32[128,1,128]{2,1,0:T(1,128)S(1)}, u32[]{:S(2)}, u32[]{:S(2)}) async-start(f32[128,1,128]{2,1,0:T(1,128)} %reshape.961), calls=%async_computation.5 | async-start | bytes 131072 | tf_op jit(solution)/shard_map/all_to_all | solution.py:66
  203.6 8.7 all-to-all-start.6
  236.4 8.9 all-to-all-start.7
  269.3 7.6 scatter_custom_fusion.8
  281.0 67.2 %all-reduce = (f32[16]{0:T(128)S(1)}, f32[16]{0:T(128)S(1)}) all-reduce(f32[16]{0:T(128)S(1)} %get-tuple-element.105, f32[16]{0:T(128)S(1)} %get-tuple-element.104), channel_id=1, replica_groups=mesh['organ'=8,'sub'=16] {'organ','sub'}, use_global_device_ids=true, to_apply=%region_13.17 | all-reduce | flops 32 | bytes 256 | tf_op jit(solution)/shard_map/psum | solution.py:118
  349.1 30.9 %psum.74 = f32[6,16]{1,0:T(8,128)S(1)} all-reduce(f32[6,16]{1,0:T(8,128)S(1)} %convolution_bitcast_fusion.3), channel_id=1, replica_groups=mesh['organ'=8,'sub'=16] {'sub'}, use_global_device_ids=true, to_apply=%region_20.24 | all-reduce | flops 96 | bytes 768 | tf_op jit(solution)/shard_map/psum | solution.py:113
  380.8 69.6 %psum.75 = f32[16]{0:T(128)S(1)} all-reduce(f32[16]{0:T(128)S(1)} %get-tuple-element.162), channel_id=1, replica_groups=mesh['organ'=8,'sub'=16] {'organ','sub'}, use_global_device_ids=true, to_apply=%region_22.26 | all-reduce | flops 16 | bytes 128 | tf_op jit(solution)/shard_map/psum | solution.py:118
  474.5 8.4 all-to-all-start.10
  484.0 7.6 scatter_custom_fusion.10
  507.7 9.8 %all-to-all-start.11 = ((f32[128,1,128]{2,1,0:T(1,128)}), f32[128,1,128]{2,1,0:T(1,128)S(1)}, u32[]{:S(2)}, u32[]{:S(2)}) async-start(f32[128,1,128]{2,1,0:T(1,128)} %reshape.973), calls=%async_computation.11 | async-start | bytes 131072 | tf_op jit(solution)/shard_map/all_to_all | solution.py:66
  541.3 7.6 scatter_custom_fusion.12
  553.7 67.2 %psum.76 = f32[16]{0:T(128)S(1)} all-reduce(f32[16]{0:T(128)S(1)} %multiply_reduce_fusion.2), channel_id=1, replica_groups=mesh['organ'=8,'sub'=16] {'organ','sub'}, use_global_device_ids=true, to_apply=%region_28.32 | all-reduce | flops 16 | bytes 128 | tf_op jit(solution)/shard_map/psum | solution.py:127
  621.9 30.9 %psum.77 = f32[6,16]{1,0:T(8,128)S(1)} all-reduce(f32[6,16]{1,0:T(8,128)S(1)} %convolution_bitcast_fusion.1), channel_id=1, replica_groups=mesh['organ'=8,'sub'=16] {'sub'}, use_global_device_ids=true, to_apply=%region_29.33 | all-reduce | flops 96 | bytes 768 | tf_op jit(solution)/shard_map/psum | solution.py:113
  653.6 69.6 %psum.78 = f32[16]{0:T(128)S(1)} all-reduce(f32[16]{0:T(128)S(1)} %get-tuple-element.164), channel_id=1, replica_groups=mesh['organ'=8,'sub'=16] {'organ','sub'}, use_global_device_ids=true, to_apply=%region_31.35 | all-reduce | flops 16 | bytes 128 | tf_op jit(solution)/shard_map/psum | solution.py:118
  746.6 8.6 all-to-all-start.14
  756.9 7.6 scatter_custom_fusion.14
  780.5 9.8 %all-to-all-start.15 = ((f32[128,1,128]{2,1,0:T(1,128)}), f32[128,1,128]{2,1,0:T(1,128)S(1)}, u32[]{:S(2)}, u32[]{:S(2)}) async-start(f32[128,1,128]{2,1,0:T(1,128)} %reshape.981), calls=%async_computation.15 | async-start | bytes 131072 | tf_op jit(solution)/shard_map/all_to_all | solution.py:66
  814.5 7.6 scatter_custom_fusion.16
  826.9 67.2 %psum.79 = f32[16]{0:T(128)S(1)} all-reduce(f32[16]{0:T(128)S(1)} %multiply_reduce_fusion), channel_id=1, replica_groups=mesh['organ'=8,'sub'=16] {'organ','sub'}, use_global_device_ids=true, to_apply=%region_37.41 | all-reduce | flops 16 | bytes 128 | tf_op jit(solution)/shard_map/psum | solution.py:127
  (418 shorter events, 308.1 us)
Async XLA Ops:
  6.5 39.5 %all-to-all-start = ((s32[128,8,1]{1,2,0:T(1,128)}), s32[128,8,1]{1,2,0:T(1,128)S(1)}, u32[]{:S(2)}, u32[]{:S(2)}) async-start(s32[128,8,1]{1,2,0:T(1,128)} %bitcast.20), calls=%async_computation | async-start | bytes 131072 | tf_op jit(solution)/shard_map/all_to_all | solution.py:55
  29.0 43.1 %collective-permute-start.3 = (f32[16,640]{1,0:T(8,128)}, f32[16,640]{1,0:T(8,128)S(1)}, u32[]{:S(2)}, u32[]{:S(2)}) collective-permute-start(f32[16,640]{1,0:T(8,128)} %bitcast.791), channel_id=1, source_target_pairs={{0,16},{16,0},{32,48},{48,32},{64,80},{80,64},{96,112},{112,96},{1... | collective-permute-start | bytes 122888 | tf_op jit(solution)/shard_map/ppermute | solution.py:13
  30.7 41.4 %collective-permute-start.4 = (f32[16,640]{1,0:T(8,128)}, f32[16,640]{1,0:T(8,128)S(1)}, u32[]{:S(2)}, u32[]{:S(2)}) collective-permute-start(f32[16,640]{1,0:T(8,128)} %bitcast.790), channel_id=1, source_target_pairs={{0,32},{16,48},{32,0},{48,16},{64,96},{80,112},{96,64},{112,80},{1... | collective-permute-start | bytes 122888 | tf_op jit(solution)/shard_map/ppermute | solution.py:13
  32.0 40.1 %collective-permute-start.1 = (f32[16,640]{1,0:T(8,128)}, f32[16,640]{1,0:T(8,128)S(1)}, u32[]{:S(2)}, u32[]{:S(2)}) collective-permute-start(f32[16,640]{1,0:T(8,128)} %bitcast.793), channel_id=1, source_target_pairs={{0,2},{1,3},{2,0},{3,1},{4,6},{5,7},{6,4},{7,5},{8,10},{9,11},{10,... | collective-permute-start | bytes 122888 | tf_op jit(solution)/shard_map/ppermute | solution.py:13
  35.3 36.8 %collective-permute-start.2 = (f32[16,640]{1,0:T(8,128)}, f32[16,640]{1,0:T(8,128)S(1)}, u32[]{:S(2)}, u32[]{:S(2)}) collective-permute-start(f32[16,640]{1,0:T(8,128)} %bitcast.792), channel_id=1, source_target_pairs={{0,4},{1,5},{2,6},{3,7},{4,0},{5,1},{6,2},{7,3},{8,12},{9,13},{10,... | collective-permute-start | bytes 122888 | tf_op jit(solution)/shard_map/ppermute | solution.py:13
  37.3 34.8 %collective-permute-start = (f32[16,640]{1,0:T(8,128)}, f32[16,640]{1,0:T(8,128)S(1)}, u32[]{:S(2)}, u32[]{:S(2)}) collective-permute-start(f32[16,640]{1,0:T(8,128)} %bitcast.794), channel_id=1, source_target_pairs={{0,1},{1,0},{2,3},{3,2},{4,5},{5,4},{6,7},{7,6},{8,9},{9,8},{10,11... | collective-permute-start | bytes 122888 | tf_op jit(solution)/shard_map/ppermute | solution.py:13
  178.2 21.4 %all-to-all-start.5 = ((f32[128,1,128]{2,1,0:T(1,128)}), f32[128,1,128]{2,1,0:T(1,128)S(1)}, u32[]{:S(2)}, u32[]{:S(2)}) async-start(f32[128,1,128]{2,1,0:T(1,128)} %reshape.961), calls=%async_computation.5 | async-start | bytes 131072 | tf_op jit(solution)/shard_map/all_to_all | solution.py:66
  190.1 22.2 %collective-permute-start.14 = (f32[16,640]{1,0:T(8,128)}, f32[16,640]{1,0:T(8,128)S(1)}, u32[]{:S(2)}, u32[]{:S(2)}) collective-permute-start(f32[16,640]{1,0:T(8,128)} %get-tuple-element.140), channel_id=1, source_target_pairs={{0,32},{16,48},{32,0},{48,16},{64,96},{80,112},{96,64},{112,80},{1... | collective-permute-start | bytes 122888 | tf_op jit(solution)/shard_map/ppermute | solution.py:13
  191.5 20.8 %collective-permute-start.13 = (f32[16,640]{1,0:T(8,128)}, f32[16,640]{1,0:T(8,128)S(1)}, u32[]{:S(2)}, u32[]{:S(2)}) collective-permute-start(f32[16,640]{1,0:T(8,128)} %get-tuple-element.141), channel_id=1, source_target_pairs={{0,16},{16,0},{32,48},{48,32},{64,80},{80,64},{96,112},{112,96},{1... | collective-permute-start | bytes 122888 | tf_op jit(solution)/shard_map/ppermute | solution.py:13
  192.1 20.2 %collective-permute-start.12 = (f32[16,640]{1,0:T(8,128)S(1)}, f32[16,640]{1,0:T(8,128)S(1)}, u32[]{:S(2)}, u32[]{:S(2)}) collective-permute-start(f32[16,640]{1,0:T(8,128)S(1)} %get-tuple-element.142), channel_id=1, source_target_pairs={{0,4},{1,5},{2,6},{3,7},{4,0},{5,1},{6,2},{7,3},{8,12},{9,13},{10,... | collective-permute-start | bytes 122888 | tf_op jit(solution)/shard_map/ppermute | solution.py:13
  246.0 21.6 %collective-permute-start.15 = (f32[16,640]{1,0:T(8,128)}, f32[16,640]{1,0:T(8,128)S(1)}, u32[]{:S(2)}, u32[]{:S(2)}) collective-permute-start(f32[16,640]{1,0:T(8,128)} %get-tuple-element.134), channel_id=1, source_target_pairs={{0,1},{1,0},{2,3},{3,2},{4,5},{5,4},{6,7},{7,6},{8,9},{9,8},{10,11... | collective-permute-start | bytes 122888 | tf_op jit(solution)/shard_map/ppermute | solution.py:13
  247.4 20.3 %collective-permute-start.19 = (f32[16,640]{1,0:T(8,128)}, f32[16,640]{1,0:T(8,128)}, u32[]{:S(2)}, u32[]{:S(2)}) collective-permute-start(f32[16,640]{1,0:T(8,128)} %get-tuple-element.135), channel_id=1, source_target_pairs={{0,32},{16,48},{32,0},{48,16},{64,96},{80,112},{96,64},{112,80},{1... | collective-permute-start | bytes 122888 | tf_op jit(solution)/shard_map/ppermute | solution.py:13
  460.6 22.3 %collective-permute-start.24 = (f32[16,640]{1,0:T(8,128)}, f32[16,640]{1,0:T(8,128)}, u32[]{:S(2)}, u32[]{:S(2)}) collective-permute-start(f32[16,640]{1,0:T(8,128)} %get-tuple-element.129), channel_id=1, source_target_pairs={{0,32},{16,48},{32,0},{48,16},{64,96},{80,112},{96,64},{112,80},{1... | collective-permute-start | bytes 122888 | tf_op jit(solution)/shard_map/ppermute | solution.py:13
  462.0 20.9 %collective-permute-start.23 = (f32[16,640]{1,0:T(8,128)}, f32[16,640]{1,0:T(8,128)}, u32[]{:S(2)}, u32[]{:S(2)}) collective-permute-start(f32[16,640]{1,0:T(8,128)} %get-tuple-element.130), channel_id=1, source_target_pairs={{0,16},{16,0},{32,48},{48,32},{64,80},{80,64},{96,112},{112,96},{1... | collective-permute-start | bytes 122888 | tf_op jit(solution)/shard_map/ppermute | solution.py:13
  462.7 20.3 %collective-permute-start.22 = (f32[16,640]{1,0:T(8,128)}, f32[16,640]{1,0:T(8,128)}, u32[]{:S(2)}, u32[]{:S(2)}) collective-permute-start(f32[16,640]{1,0:T(8,128)} %get-tuple-element.131), channel_id=1, source_target_pairs={{0,4},{1,5},{2,6},{3,7},{4,0},{5,1},{6,2},{7,3},{8,12},{9,13},{10,... | collective-permute-start | bytes 122888 | tf_op jit(solution)/shard_map/ppermute | solution.py:13
  507.7 21.0 %all-to-all-start.11 = ((f32[128,1,128]{2,1,0:T(1,128)}), f32[128,1,128]{2,1,0:T(1,128)S(1)}, u32[]{:S(2)}, u32[]{:S(2)}) async-start(f32[128,1,128]{2,1,0:T(1,128)} %reshape.973), calls=%async_computation.11 | async-start | bytes 131072 | tf_op jit(solution)/shard_map/all_to_all | solution.py:66
  518.1 21.4 %collective-permute-start.25 = (f32[16,640]{1,0:T(8,128)}, f32[16,640]{1,0:T(8,128)}, u32[]{:S(2)}, u32[]{:S(2)}) collective-permute-start(f32[16,640]{1,0:T(8,128)} %get-tuple-element.123), channel_id=1, source_target_pairs={{0,1},{1,0},{2,3},{3,2},{4,5},{5,4},{6,7},{7,6},{8,9},{9,8},{10,11... | collective-permute-start | bytes 122888 | tf_op jit(solution)/shard_map/ppermute | solution.py:13
  519.5 20.1 %collective-permute-start.29 = (f32[16,640]{1,0:T(8,128)}, f32[16,640]{1,0:T(8,128)}, u32[]{:S(2)}, u32[]{:S(2)}) collective-permute-start(f32[16,640]{1,0:T(8,128)} %get-tuple-element.124), channel_id=1, source_target_pairs={{0,32},{16,48},{32,0},{48,16},{64,96},{80,112},{96,64},{112,80},{1... | collective-permute-start | bytes 122888 | tf_op jit(solution)/shard_map/ppermute | solution.py:13
  732.9 22.3 %collective-permute-start.34 = (f32[16,640]{1,0:T(8,128)}, f32[16,640]{1,0:T(8,128)S(1)}, u32[]{:S(2)}, u32[]{:S(2)}) collective-permute-start(f32[16,640]{1,0:T(8,128)} %get-tuple-element.118), channel_id=1, source_target_pairs={{0,32},{16,48},{32,0},{48,16},{64,96},{80,112},{96,64},{112,80},{1... | collective-permute-start | bytes 122888 | tf_op jit(solution)/shard_map/ppermute | solution.py:13
  734.2 20.9 %collective-permute-start.33 = (f32[16,640]{1,0:T(8,128)}, f32[16,640]{1,0:T(8,128)S(1)}, u32[]{:S(2)}, u32[]{:S(2)}) collective-permute-start(f32[16,640]{1,0:T(8,128)} %get-tuple-element.119), channel_id=1, source_target_pairs={{0,16},{16,0},{32,48},{48,32},{64,80},{80,64},{96,112},{112,96},{1... | collective-permute-start | bytes 122888 | tf_op jit(solution)/shard_map/ppermute | solution.py:13
  735.1 20.1 %collective-permute-start.32 = (f32[16,640]{1,0:T(8,128)}, f32[16,640]{1,0:T(8,128)S(1)}, u32[]{:S(2)}, u32[]{:S(2)}) collective-permute-start(f32[16,640]{1,0:T(8,128)} %get-tuple-element.120), channel_id=1, source_target_pairs={{0,4},{1,5},{2,6},{3,7},{4,0},{5,1},{6,2},{7,3},{8,12},{9,13},{10,... | collective-permute-start | bytes 122888 | tf_op jit(solution)/shard_map/ppermute | solution.py:13
  780.5 21.1 %all-to-all-start.15 = ((f32[128,1,128]{2,1,0:T(1,128)}), f32[128,1,128]{2,1,0:T(1,128)S(1)}, u32[]{:S(2)}, u32[]{:S(2)}) async-start(f32[128,1,128]{2,1,0:T(1,128)} %reshape.981), calls=%async_computation.15 | async-start | bytes 131072 | tf_op jit(solution)/shard_map/all_to_all | solution.py:66
  791.0 21.7 %collective-permute-start.35 = (f32[16,640]{1,0:T(8,128)}, f32[16,640]{1,0:T(8,128)}, u32[]{:S(2)}, u32[]{:S(2)}) collective-permute-start(f32[16,640]{1,0:T(8,128)} %get-tuple-element.112), channel_id=1, source_target_pairs={{0,1},{1,0},{2,3},{3,2},{4,5},{5,4},{6,7},{7,6},{8,9},{9,8},{10,11... | collective-permute-start | bytes 122888 | tf_op jit(solution)/shard_map/ppermute | solution.py:13
  792.4 20.3 %collective-permute-start.39 = (f32[16,640]{1,0:T(8,128)}, f32[16,640]{1,0:T(8,128)}, u32[]{:S(2)}, u32[]{:S(2)}) collective-permute-start(f32[16,640]{1,0:T(8,128)} %get-tuple-element.113), channel_id=1, source_target_pairs={{0,32},{16,48},{32,0},{48,16},{64,96},{80,112},{96,64},{112,80},{1... | collective-permute-start | bytes 122888 | tf_op jit(solution)/shard_map/ppermute | solution.py:13
  (74 other events, 1861.5 us)
where the time goes:
time: 905 us; the launch traced here: 896 us
  blocking collectives  436 us (48%)
  starting transfers between devices  192 us (21%)
  local copies, waits for them, and re-layouts  98.9 us (11%)
  other arithmetic  95.8 us (11%)
  matrix products  49.5 us (5%)
  between operations  12.8 us (1%)
  waiting for transfers between devices  10 us (1%)
    psum x3, blocking collectives, project(): lax.psum(jnp.sum(resid * projected, axis=(1, 2)), ('organ', 'sub'))  206 us
    psum x2, blocking collectives, local(): lax.psum(jnp.sum(direction * image, axis=(1, 2)), ('organ', 'sub'))  134 us
    all_to_all x16, starting transfers between devices, route(): lax.all_to_all(outgoing, ('organ', 'sub'), split_axis=1, concat_axis=1, t...  124 us
    psum x3, blocking collectives, project(): coeffs = lax.psum(coeff_local, 'sub')  95.7 us
    scatter-add x8, other arithmetic, contact_term(): jnp.zeros((directions, block_len), jnp.float32).at[:, incoming_index]  58.6 us
    ppermute x40, starting transfers between devices, from_partner(): return lax.ppermute(value, axis, pairs)  56.4 us
    dot_general x4, matrix products, operator(): jnp.einsum('kbn,bnm->kbm', inner, matrices, precision=lax.Precision.HIGHEST)  29.1 us
    unnamed x129, local copies, waits for them, and re-layouts  29.1 us
  transfers between devices with their start and end apart: 57, of which 4 were waited for; matrix products, arithmetic and copies ran while one was open for 16% of the time, Pallas kernels for 0%

commit v1 on v0

v1 whole, which is shorter than its diff:
```python
import jax
import jax.numpy as jnp
from jax import lax
from jax.experimental import pallas as pl
from jax.experimental.pallas import tpu as pltpu
from jax.sharding import PartitionSpec as P

ITERS = 3
CAP = 8
MESH = pl.DeviceIdType.MESH
F32 = jnp.float32
BF16 = jnp.bfloat16
N_ORG, N_SUB = 8, 16
N_DEV = N_ORG * N_SUB
LANES = 128
ROWS = (1, 4, 3, 3, 3, 3, 3, 3, 1)
N_ROUND = len(ROWS)
N_MATCH = 5
N_HALO = 2 * ITERS + 1


def iota(shape, dim):
    return lax.broadcasted_iota(jnp.int32, shape, dim)


def split3(x):
    high = x.astype(BF16)
    rest = x - high.astype(F32)
    mid = rest.astype(BF16)
    low = (rest - mid.astype(F32)).astype(BF16)
    return high, mid, low


def split2(x):
    high = x.astype(BF16)
    return high, (x - high.astype(F32)).astype(BF16)


def dot(a, b):
    return jnp.dot(a, b, preferred_element_type=F32)


def mm(x, w_high, w_low):
    n = x.shape[0]
    high, mid, low = split3(x)
    a = dot(jnp.concatenate([high, mid, low], axis=0), w_high)
    b = dot(jnp.concatenate([high, mid], axis=0), w_low)
    return a[:n] + (a[n : 2 * n] + b[:n] + (a[2 * n :] + b[n:]))


def offset_of(u):
    return u - (u // 2) * (2 * u - 5)


def kernel(
    rhs_hbm,
    warm_hbm,
    inv_hbm,
    coarse_hbm,
    mortar_hbm,
    owner_ref,
    dofs_ref,
    active_ref,
    rounds_ref,
    counts_ref,
    out_hbm,
    g_stage,
    g_high,
    g_low,
    m_stage,
    pick_ref,
    wf_high,
    wf_low,
    wb_high,
    wb_low,
    wt_high,
    wt_low,
    q_ref,
    qt_ref,
    p_ref,
    d_ref,
    w_ref,
    y_ref,
    yp_ref,
    ym_ref,
    r_ref,
    sol_ref,
    q_stage,
    x_stage,
    r_stage,
    msend,
    qsend,
    qrecv,
    *rest,
):
    sends, recvs = rest[:N_ROUND], rest[N_ROUND : 2 * N_ROUND]
    mrecv = rest[2 * N_ROUND : 2 * N_ROUND + N_HALO]
    (load_sem, out_sem, send_sem, recv_sem, self_sem, ms_sem, mr_sem, qs_sem, qr_sem) = rest[
        2 * N_ROUND + N_HALO :
    ]
    faces, dirs, length = p_ref.shape
    rows = m_stage.shape[0]
    modes = coarse_hbm.shape[0]
    slots = CAP * N_DEV
    org, sub = lax.axis_index("organ"), lax.axis_index("sub")
    me = org * N_SUB + sub
    x_at, core_at, z_at, y_at = org // 2, org % 2, sub // 4, sub % 4

    def peer(i):
        u = N_DEV - 1 - i
        px = (x_at + offset_of(u // 32)) % 4
        pc = (core_at + (u // 16) % 2) % 2
        pz = (z_at + offset_of((u // 4) % 4)) % 4
        py = (y_at + offset_of(u % 4)) % 4
        return px * 2 + pc, pz * 4 + py

    barrier = pltpu.get_barrier_semaphore()

    def greet(i, carry):
        pl.semaphore_signal(barrier, inc=1, device_id=peer(i), device_id_type=MESH)
        return carry

    lax.fori_loop(0, N_DEV - 1, greet, 0)

    loads = [pltpu.make_async_copy(mortar_hbm, m_stage, load_sem.at[0])]
    q_ref[...] = jnp.zeros(q_ref.shape, F32)
    qt_ref[...] = jnp.zeros(qt_ref.shape, F32)
    q_loads = [pltpu.make_async_copy(coarse_hbm, q_stage, load_sem.at[1])]
    x_loads = [pltpu.make_async_copy(warm_hbm, x_stage, load_sem.at[6])]
    r_loads = [pltpu.make_async_copy(rhs_hbm, r_stage, load_sem.at[11])]
    g_loads = [
        pltpu.make_async_copy(inv_hbm.at[f], g_stage.at[f], load_sem.at[16 + f])
        for f in range(faces)
    ]
    for copy in loads + q_loads + x_loads + r_loads + g_loads:
        copy.start()

    def start_round(i):
        n = ROWS[i]
        sb, rb = sends[i], recvs[i]

        def go(step, carry):
            po, ps = peer(step)
            pltpu.make_async_remote_copy(
                sb.at[pl.ds((po * N_SUB + ps) * n, n)],
                rb.at[pl.ds(me * n, n)],
                send_sem.at[i],
                recv_sem.at[i],
                device_id=(po, ps),
                device_id_type=MESH,
            ).start()
            return carry

        lax.fori_loop(0, N_DEV - 1, go, 0)
        pltpu.make_async_copy(
            sb.at[pl.ds(me * n, n)], rb.at[pl.ds(me * n, n)], self_sem.at[i]
        ).start()

    def wait_round(i):
        n = ROWS[i]
        sb, rb = sends[i], recvs[i]
        pltpu.make_async_copy(
            sb.at[pl.ds(me * n, n)], rb.at[pl.ds(me * n, n)], self_sem.at[i]
        ).wait()
        most = pl.ds(0, (N_DEV - 1) * n)
        pltpu.make_async_copy(rb.at[most], rb.at[most], recv_sem.at[i]).wait()
        pltpu.make_async_copy(sb.at[most], sb.at[most], send_sem.at[i]).wait()

    def put(i, j, value):
        sends[i][pl.ds(j, N_DEV, stride=ROWS[i]), :] = value

    def got(i, j):
        return recvs[i][pl.ds(j, N_DEV, stride=ROWS[i]), :]

    def partners():
        out = []
        for r in range(3):
            step = 2**r
            out.append((org, sub + step * (1 - 2 * ((sub // step) % 2))))
        for r in range(2):
            step = 2**r
            out.append((org + step * (1 - 2 * ((org // step) % 2)), sub))
        return out

    face_of = [rounds_ref[0, r] for r in range(N_MATCH)]
    round_of = []
    for f in range(faces):
        found = jnp.int32(0)
        for r in range(1, N_MATCH):
            found = jnp.where(face_of[r] == f, r, found)
        round_of.append(found)

    def start_match(source, send, recv, s_sem, r_sem):
        copies = []
        for r, dev in enumerate(partners()):
            send[r] = source[face_of[r]]
        for r, dev in enumerate(partners()):
            copy = pltpu.make_async_remote_copy(
                send.at[r], recv.at[r], s_sem.at[r], r_sem.at[r], device_id=dev, device_id_type=MESH
            )
            copy.start()
            copies.append(copy)
        return copies

    live = (active_ref[...] > 0) & (iota((1, rows), 1) < counts_ref[0, 0])
    owner = jnp.where(live, owner_ref[...], -1)
    owned = iota((N_DEV, rows), 0) == owner
    before = (iota((rows, rows), 0) < iota((rows, rows), 1)).astype(F32).astype(BF16)
    earlier = dot(owned.astype(F32).astype(BF16), before)
    rank = jnp.sum(jnp.where(owned, earlier, 0.0), axis=0, keepdims=True).astype(jnp.int32)
    slot = jnp.where(live, rank * N_DEV + owner, -1)
    dof_plus = dofs_ref[...].astype(F32) + 1.0
    lane = iota((N_DEV, LANES), 1)
    table = jnp.zeros((N_DEV, LANES), F32)
    for k in range(CAP):
        chosen = iota((N_DEV, rows), 0) + k * N_DEV == slot
        pick_ref[k] = chosen.astype(F32).astype(BF16)
        column = jnp.sum(jnp.where(chosen, dof_plus, 0.0), axis=1, keepdims=True) - 1.0
        table = jnp.where(lane == k, column, table)

    for copy in q_loads:
        copy.wait()
    for f in range(faces):
        q_ref[f, :modes] = q_stage[:, f, :]
    gram = jnp.zeros((8, LANES), F32)
    for f in range(faces):
        own = q_ref[f, :8]
        tiled = jnp.concatenate([own] * (LANES // 8), axis=0)
        gram = gram + lax.dot_general(
            own, tiled, (((1,), (1,)), ((), ())), precision=lax.Precision.HIGHEST,
            preferred_element_type=F32,
        )
    keep = iota((8, LANES), 1) // 8 == iota((8, LANES), 0) + 8
    table = table + jnp.sum(jnp.where(keep, gram, 0.0), axis=0, keepdims=True)
    put(0, 0, table)
    pl.semaphore_wait(barrier, N_DEV - 1)
    start_round(0)

    for copy in loads:
        copy.wait()
    m_high, m_low = split2(m_stage[...])

    def arrange(k, carry):
        at = pl.ds(pl.multiple_of(k * N_DEV, N_DEV), N_DEV)
        for part, back, ahead in ((m_high, wb_high, wf_high), (m_low, wb_low, wf_low)):
            block = dot(pick_ref[k], part)
            back[at, :] = block.astype(BF16)
            ahead[:, at] = block.T.astype(BF16)
        return carry

    lax.fori_loop(0, CAP, arrange, 0)

    eye = [iota((dirs, LANES), 1) == iota((dirs, LANES), 0) + dirs * m for m in range(8)]

    def to_row(columns):
        total = jnp.zeros((dirs, LANES), F32)
        for m, column in columns:
            total = total + jnp.where(eye[m], column, 0.0)
        return jnp.sum(total, axis=0, keepdims=True)

    def to_column(row, m):
        return jnp.sum(jnp.where(eye[m], row, 0.0), axis=1, keepdims=True)

    def inner(a_ref, b_ref):
        total = a_ref[0] * b_ref[0]
        for f in range(1, faces):
            total = total + a_ref[f] * b_ref[f]
        return jnp.sum(total, axis=1, keepdims=True)

    for copy in r_loads:
        copy.wait()
    for f in range(faces):
        r_ref[f] = r_stage[:, f, :]
    rhs_modes = []
    for m in range(modes):
        total = r_ref[0] * q_ref[0, m : m + 1]
        for f in range(1, faces):
            total = total + r_ref[f] * q_ref[f, m : m + 1]
        rhs_modes.append((m, jnp.sum(total, axis=1, keepdims=True)))
    rhs_row = to_row(rhs_modes)

    for copy in x_loads:
        copy.wait()
    for f in range(faces):
        p_ref[f] = x_stage[:, f, :]
    copies = start_match(p_ref, msend.at[0], mrecv[0], ms_sem.at[0], mr_sem.at[0])
    for r in range(N_MATCH):
        qsend[r] = q_ref[face_of[r], :8]
    q_copies = []
    for r, dev in enumerate(partners()):
        copy = pltpu.make_async_remote_copy(
            qsend.at[r], qrecv.at[r], qs_sem.at[r], qr_sem.at[r], device_id=dev, device_id_type=MESH
        )
        copy.start()
        q_copies.append(copy)

    wait_round(0)
    table = recvs[0][...]
    table_t = table.T
    in_group = iota((N_DEV, LANES), 0) // N_SUB == org
    gram_row = jnp.sum(jnp.where(in_group, table, 0.0), axis=0, keepdims=True)
    for k in range(CAP):
        column = table[:, k : k + 1].astype(jnp.int32)
        hit = iota((N_DEV, length), 1) == column
        wb_high[slots + k * N_DEV : slots + (k + 1) * N_DEV, :] = jnp.where(hit, -1.0, 0.0).astype(BF16)
        hit = iota((length, N_DEV), 0) == table_t[k : k + 1, :].astype(jnp.int32)
        wf_high[:, slots + k * N_DEV : slots + (k + 1) * N_DEV] = jnp.where(hit, 1.0, 0.0).astype(BF16)

    def row_values(x):
        n = x.shape[0]
        high, mid, low = split3(x)
        full = dot(jnp.concatenate([high, mid, low], axis=0), wf_high[...])
        fine = dot(jnp.concatenate([high, mid], axis=0), wf_low[...])
        full = full[:n] + (full[n : 2 * n] + full[2 * n :])
        return full[:, :slots] + (fine[:n] + fine[n:]), full[:, slots:]

    def spread_gaps(gaps):
        n = gaps.shape[0]
        high, mid, low = split3(gaps)
        full = dot(jnp.concatenate([high, mid, low], axis=0), wb_high[...])
        fine = dot(jnp.concatenate([high[:, :slots], mid[:, :slots]], axis=0), wb_low[...])
        return full[:n] + (full[n : 2 * n] + fine[:n] + (full[2 * n :] + fine[n:]))

    def stacked(value):
        return jnp.concatenate(
            [value[:, k * N_DEV : (k + 1) * N_DEV] for k in range(CAP)], axis=0
        )

    def unstacked(value):
        n = value.shape[0] // CAP
        return jnp.concatenate([value[k * n : (k + 1) * n] for k in range(CAP)], axis=1)

    def face_gaps(i, mine_a, mine_s):
        theirs_a, theirs_s = got(i, 0).T, got(i, 1).T
        return jnp.concatenate(
            [unstacked(mine_a - theirs_s), unstacked(theirs_a - mine_s)], axis=1
        )

    both_a, both_s = row_values(jnp.concatenate([p_ref[0], q_ref[0]], axis=0))
    mine_a, mine_s = stacked(both_a[:dirs]), stacked(both_s[:dirs])
    qa, qs = both_a[dirs : dirs + 8], both_s[dirs : dirs + 8]
    put(1, 0, mine_a.T)
    put(1, 1, mine_s.T)
    put(1, 2, jnp.broadcast_to(rhs_row, (N_DEV, LANES)))
    put(1, 3, jnp.concatenate([stacked(qa), stacked(qs)], axis=0).T)
    start_round(1)

    def gram_at(i, j):
        at = 64 + 8 * i + j
        return gram_row[:, at : at + 1]

    factor, inverse = {}, []
    for j in range(modes):
        pivot = gram_at(j, j)
        for k in range(j):
            pivot = pivot - factor[j, k] * factor[j, k]
        pivot = jnp.sqrt(pivot)
        inverse.append(1.0 / pivot)
        for i in range(j + 1, modes):
            value = gram_at(i, j)
            for k in range(j):
                value = value - factor[i, k] * factor[j, k]
            factor[i, j] = value * inverse[j]
    for f in range(faces):
        made = []
        for i in range(modes):
            row = q_ref[f, i : i + 1]
            for k in range(i):
                row = row - factor[i, k] * made[k]
            made.append(row * inverse[i])
            qt_ref[f, i : i + 1] = made[i]

    chunk = 64
    for f in range(faces):
        g_loads[f].wait()

        def halve(i, carry, f=f):
            at = pl.ds(pl.multiple_of(i * chunk, chunk), chunk)
            high, low = split2(g_stage[f, at, :])
            g_high[f, at, :] = high
            g_low[f, at, :] = low
            return carry

        lax.fori_loop(0, length // chunk, halve, 0)

    rho = None
    c_res = None
    for t in range(ITERS + 1):
        a_round = 1 + 2 * t
        for copy in copies:
            copy.wait()
        halo = mrecv[2 * t]
        for f in range(faces):
            yp_ref[f] = p_ref[f] - halo[round_of[f]]

        def smooth_face(f, carry):
            ym_ref[f] = mm(
                yp_ref[f], g_high[f], g_low[f]
            )
            return carry

        lax.fori_loop(1, faces, smooth_face, 0)

        wait_round(a_round)
        gaps = face_gaps(a_round, mine_a, mine_s)
        if t == 0:
            for copy in q_copies:
                copy.wait()
            c_row = jnp.sum(jnp.where(in_group, got(1, 2), 0.0), axis=0, keepdims=True)
            c_res = [to_column(c_row, m) for m in range(modes)]
            theirs = got(1, 3).T
            organ_row = iota((8, LANES), 0)
            of_peer = iota((8, LANES), 1) // N_SUB == organ_row
            mine = organ_row == org
            blocks = []
            for m in range(modes):
                outs, ins = [], []
                for k in range(CAP):
                    at = slice(k * N_DEV, (k + 1) * N_DEV)
                    ta = theirs[k * 8 + m : k * 8 + m + 1]
                    ts = theirs[64 + k * 8 + m : 64 + k * 8 + m + 1]
                    outs.append(
                        jnp.where(mine, qa[m : m + 1, at], 0.0) - jnp.where(of_peer, ts, 0.0)
                    )
                    ins.append(
                        jnp.where(of_peer, ta, 0.0) - jnp.where(mine, qs[m : m + 1, at], 0.0)
                    )
                blocks.append(jnp.concatenate(outs + ins, axis=1))
            mode_gaps = jnp.concatenate(blocks, axis=0)
            both = spread_gaps(jnp.concatenate([gaps, mode_gaps], axis=0))
            contact, mode_contact = both[:dirs], both[dirs:]
            organ_col = iota((8, length), 0)
            for f in range(faces):
                at_round = round_of[f]
                other = jnp.where(
                    at_round < 3,
                    org,
                    jnp.where(
                        at_round == 3, org + 1 - 2 * (org % 2), org + 2 - 4 * ((org // 2) % 2)
                    ),
                )
                arrived = qrecv[at_round]
                parts = []
                for m in range(modes):
                    part = jnp.where(organ_col == org, q_ref[f, m : m + 1], 0.0) - jnp.where(
                        organ_col == other, arrived[m : m + 1], 0.0
                    )
                    if f == 0:
                        part = part + mode_contact[8 * m : 8 * m + 8]
                    parts.append(part)
                parts.append(jnp.zeros((LANES - 8 * modes, length), F32))
                wide = jnp.concatenate(parts, axis=0).T
                high, low = split2(wide)
                wt_high[f] = high
                wt_low[f] = low
        else:
            contact = spread_gaps(gaps)
            rho_new = to_column(jnp.sum(got(a_round, 2), axis=0, keepdims=True), 0)
            beta = rho_new / rho if t > 1 else None
            rho = rho_new
        yp_ref[0] = yp_ref[0] + contact
        ym_ref[0] = mm(yp_ref[0], g_high[0], g_low[0])

        for f in range(faces):
            made = ym_ref[f]
            if t > 1:
                w_ref[f] = yp_ref[f] + beta * w_ref[f]
                y_ref[f] = made + beta * y_ref[f]
                d_ref[f] = p_ref[f] + beta * d_ref[f]
            else:
                w_ref[f] = yp_ref[f]
                y_ref[f] = made
                d_ref[f] = p_ref[f]
        curved = inner(w_ref, y_ref)

        b_round = a_round + 1
        if t == ITERS:
            put(b_round, 0, jnp.broadcast_to(to_row([(0, curved)]), (N_DEV, LANES)))
            start_round(b_round)
            wait_round(b_round)
            step = rho / to_column(jnp.sum(recvs[b_round][...], axis=0, keepdims=True), 0)
            for f in range(faces):
                sol_ref[f] = sol_ref[f] + step * d_ref[f]
            break

        copies = start_match(
            y_ref, msend.at[2 * t + 1], mrecv[2 * t + 1], ms_sem.at[2 * t + 1], mr_sem.at[2 * t + 1]
        )
        mine_a, mine_s = row_values(y_ref[0])
        mine_a, mine_s = stacked(mine_a), stacked(mine_s)
        put(b_round, 0, mine_a.T)
        put(b_round, 1, mine_s.T)
        coarse = mm(y_ref[0], wt_high[0], wt_low[0])
        for f in range(1, faces):
            coarse = coarse + mm(y_ref[f], wt_high[f], wt_low[f])
        coarse = jnp.concatenate([coarse, jnp.zeros((LANES - dirs, LANES), F32)], axis=0).T
        parts = [coarse[8 * m : 8 * m + 8, :dirs] for m in range(modes)]
        parts.append(jnp.zeros((8, LANES - modes * dirs), F32))
        coarse = jnp.concatenate(parts, axis=1) + to_row([(modes, curved)])
        for o in range(N_ORG):
            sends[b_round][pl.ds(o * N_SUB * ROWS[b_round] + 2, N_SUB, stride=ROWS[b_round]), :] = (
                jnp.broadcast_to(coarse[o : o + 1], (N_SUB, LANES))
            )
        start_round(b_round)

        for copy in copies:
            copy.wait()
        halo = mrecv[2 * t + 1]
        for f in range(faces):
            yp_ref[f] = y_ref[f] - halo[round_of[f]]
        wait_round(b_round)
        yp_ref[0] = yp_ref[0] + spread_gaps(face_gaps(b_round, mine_a, mine_s))
        total = jnp.sum(got(b_round, 2), axis=0, keepdims=True)
        c_image = [to_column(total, m) for m in range(modes)]
        if t > 0:
            step = rho / to_column(total, modes)
        for f in range(faces):
            if t > 0:
                sol_ref[f] = sol_ref[f] + step * d_ref[f]
                r_ref[f] = r_ref[f] - step * yp_ref[f]
            else:
                sol_ref[f] = d_ref[f]
                r_ref[f] = r_ref[f] - yp_ref[f]
        for m in range(modes):
            c_res[m] = c_res[m] - (step * c_image[m] if t > 0 else c_image[m])
        solved = []
        for i in range(modes):
            value = c_res[i]
            for k in range(i):
                value = value - factor[i, k] * solved[k]
            solved.append(value * inverse[i])
        for f in range(faces):
            value = r_ref[f]
            for m in range(modes):
                value = value - solved[m] * qt_ref[f, m : m + 1]
            p_ref[f] = value

        n_halo = 2 * t + 2
        copies = start_match(
            p_ref, msend.at[n_halo], mrecv[n_halo], ms_sem.at[n_halo], mr_sem.at[n_halo]
        )
        mine_a, mine_s = row_values(p_ref[0])
        mine_a, mine_s = stacked(mine_a), stacked(mine_s)
        put(b_round + 1, 0, mine_a.T)
        put(b_round + 1, 1, mine_s.T)
        put(
            b_round + 1,
            2,
            jnp.broadcast_to(to_row([(0, inner(r_ref, p_ref))]), (N_DEV, LANES)),
        )
        start_round(b_round + 1)

    for f in range(faces):
        x_stage[:, f, :] = sol_ref[f]
    write = pltpu.make_async_copy(x_stage, out_hbm, out_sem.at[0])
    write.start()
    write.wait()


def local(
    dual_rhs,
    warm_start,
    inverse_blocks,
    coarse_basis,
    mortar_rows,
    match_rounds,
    slave_owner,
    slave_dofs,
    active_set,
    row_counts,
):
    dirs, _, _, faces, length = dual_rhs.shape
    rows = mortar_rows.shape[2]
    modes = coarse_basis.shape[0]
    slots = CAP * N_DEV
    field = pltpu.VMEM((faces, dirs, length), F32)
    dma = pltpu.SemaphoreType.DMA
    any_spec = pl.BlockSpec(memory_space=pl.ANY)
    vmem_spec = pl.BlockSpec(memory_space=pltpu.VMEM)
    smem_spec = pl.BlockSpec(memory_space=pltpu.SMEM)
    scratch = [
        pltpu.VMEM((faces, length, length), F32),
        pltpu.VMEM((faces, length, length), BF16),
        pltpu.VMEM((faces, length, length), BF16),
        pltpu.VMEM((rows, length), F32),
        pltpu.VMEM((CAP, N_DEV, rows), BF16),
        pltpu.VMEM((length, 2 * slots), BF16),
        pltpu.VMEM((length, slots), BF16),
        pltpu.VMEM((2 * slots, length), BF16),
        pltpu.VMEM((slots, length), BF16),
        pltpu.VMEM((faces, length, LANES), BF16),
        pltpu.VMEM((faces, length, LANES), BF16),
        field,
        pltpu.VMEM((faces, 8, length), F32),
    ]
    scratch += [field] * 8
    scratch += [
        pltpu.VMEM((modes, faces, length), F32),
        pltpu.VMEM((dirs, faces, length), F32),
        pltpu.VMEM((dirs, faces, length), F32),
        pltpu.VMEM((N_HALO, N_MATCH, dirs, length), F32),
        pltpu.VMEM((N_MATCH, 8, length), F32),
        pltpu.VMEM((N_MATCH, 8, length), F32),
    ]
    scratch += [pltpu.VMEM((N_DEV * n, LANES), F32) for n in ROWS] * 2
    scratch += [pltpu.VMEM((N_MATCH, dirs, length), F32)] * N_HALO
    scratch += [
        dma((21,)),
        dma((faces,)),
        dma((N_ROUND,)),
        dma((N_ROUND,)),
        dma((N_ROUND,)),
        dma((N_HALO, N_MATCH)),
        dma((N_HALO, N_MATCH)),
        dma((N_MATCH,)),
        dma((N_MATCH,)),
    ]
    result = pl.pallas_call(
        kernel,
        out_shape=jax.ShapeDtypeStruct((dirs, faces, length), F32),
        in_specs=[any_spec] * 5 + [vmem_spec] * 3 + [smem_spec] * 2,
        out_specs=any_spec,
        scratch_shapes=scratch,
        compiler_params=pltpu.CompilerParams(
            collective_id=0, has_side_effects=True, vmem_limit_bytes=60 * 2**20
        ),
    )(
        dual_rhs.reshape(dirs, faces, length),
        warm_start.reshape(dirs, faces, length),
        inverse_blocks.reshape(faces, length, length),
        coarse_basis.reshape(modes, faces, length),
        mortar_rows.reshape(rows, length),
        slave_owner.reshape(1, rows),
        slave_dofs.reshape(1, rows),
        active_set.reshape(1, rows),
        match_rounds.reshape(1, N_MATCH),
        row_counts.reshape(1, 1),
    )
    return result.reshape(dirs, 1, 1, faces, length)


def solution(mesh):
    in_specs = (
        P(None, "organ", "sub", None, None),
        P(None, "organ", "sub", None, None),
        P("organ", "sub", None, None, None),
        P(None, "organ", "sub", None, None),
        P("organ", "sub", None, None),
        P("organ", "sub", None),
        P("organ", "sub", None, None),
        P("organ", "sub", None),
        P("organ", "sub", None),
        P("organ", "sub", None),
    )
    out_specs = P(None, "organ", "sub", None, None)
    return jax.shard_map(local, mesh=mesh, in_specs=in_specs, out_specs=out_specs, check_vma=False)
```

time: 905 us -> 138 us (0.15)
  blocking collectives: 436 us -> 0 us
  starting transfers between devices: 192 us -> 0 us
  Pallas kernels: 0 us -> 131 us
  other arithmetic: 95.8 us -> 0 us
  local copies, waits for them, and re-layouts: 98.9 us -> 5.38 us
  matrix products: 49.5 us -> 0 us
  between operations: 12.8 us -> 0.66 us
  waiting for transfers between devices: 10 us -> 0 us
    psum x8 -> x0, blocking collectives: 436 us -> none  [the longest x3 206 us: project(): lax.psum(jnp.sum(resid * projected, axis=(1, 2)), ('organ', 'sub'))]
    all_to_all x17 -> x0, starting transfers between devices: 136 us -> none  [the longest x16 124 us: route(): lax.all_to_all(outgoing, ('organ', 'sub'), split_axis=1, concat_axis=1, t...]
    pallas_call x0 -> x1, Pallas kernels: none -> 131 us  [local(): pl.pallas_call(kernel, out_shape=jax.ShapeDtypeStruct((dirs, faces, lengt...]
    scatter-add x8 -> x0, other arithmetic: 58.6 us -> none  [contact_term(): jnp.zeros((directions, block_len), jnp.float32).at[:, incoming_index]]
    ppermute x40 -> x0, starting transfers between devices: 56.4 us -> none  [from_partner(): return lax.ppermute(value, axis, pairs)]
    dot_general x27 -> x0, matrix products: 48.5 us -> none  [the longest x4 29.1 us: operator(): jnp.einsum('kbn,bnm->kbm', inner, matrices, precision=lax.Precision.HIGHEST)]
    gather x16 -> x0, local copies, waits for them, and re-layouts: 30.8 us -> none  [the longest x8 22.5 us: contact_term(): slave_vals = jnp.take(surface, incoming_index, axis=1)]
    unnamed x129 -> x0, local copies, waits for them, and re-layouts: 29.1 us -> none
  transfers between devices with their start and end apart: 57 -> 0, of which waited for: 4 -> 0; matrix products, arithmetic and copies ran while one was open for 16% -> 0% of each run, Pallas kernels for 0% -> 0%
where the time goes in v1:
time: 138 us; the launch traced here: 137 us
  Pallas kernels  131 us (95%)
  local copies, waits for them, and re-layouts  5.38 us (4%)
    pallas_call x1, Pallas kernels, local(): pl.pallas_call(kernel, out_shape=jax.ShapeDtypeStruct((dirs, faces, lengt...  131 us

profile of v1, /device:TPU:1, one launch (start us, length us, event | category | flops | bytes accessed | tf_op | source)
XLA Modules:
  0.0 137.5 jit_solution(1629126652161554013)
XLA Ops:
  0.7 1.6 %copy.25 = f32[6,1,1,5,640]{4,3,0,1,2:T(8,128)} copy(f32[6,1,1,5,640]{4,2,3,1,0:T(1,128)} %param.13) | data formatting | bytes 153600 | tf_op jit(solution)/shard_map/reshape | solution.py:631
  2.2 2.0 %copy_bitcast_fusion = (f32[16,5,640]{2,1,0:T(8,128)}, f32[16,5,640]{2,1,0:T(8,128)}) fusion(f32[16,1,1,5,640]{4,2,3,1,0:T(1,128)} %param.11, f32[16,1,1,5,640]{4,2,3,1,0:T(1,128)} %param.10), kind=kLoop, calls=%fused_computation | loop fusion | bytes 819200 | tf_op jit(solution)/shard_map/reshape | solution.py:629
  4.2 131.5 %shard_map.100 = f32[16,5,640]{2,1,0:T(8,128)} custom-call(f32[16,5,640]{2,1,0:T(8,128)} %get-tuple-element.6.rhs_hbm, f32[16,5,640]{2,1,0:T(8,128)} %get-tuple-element.5.warm_hbm, f32[5,640,640]{2,1,0:T(8,128)} %bitcast.19, f32[6,5,640]{2,1,0:T(8,128)} %bitcast.22, f32[512,640]{1,0:T(8,128)} %bitcast.21, s32[1,512]{1,0:T(1,128)} %bitcast.23, ...), custom_call_target="tpu_custom_call" | custom-call | tf_op jit(solution)/shard_map/pallas_call | solution.py:618
  135.6 1.9 %copy.18 = f32[16,1,1,5,640]{4,2,3,1,0:T(1,128)} copy(f32[16,1,1,5,640]{4,3,0,2,1:T(8,128)} %bitcast.20) | data formatting | bytes 409600 | tf_op jit(solution)/shard_map/reshape | solution.py:639

commit v2 on v1

--- a/solution.py
+++ b/solution.py
@@ -106,21 +106,26 @@
     me = org * N_SUB + sub
     x_at, core_at, z_at, y_at = org // 2, org % 2, sub // 4, sub % 4
 
-    def peer(i):
-        u = N_DEV - 1 - i
-        px = (x_at + offset_of(u // 32)) % 4
-        pc = (core_at + (u // 16) % 2) % 2
-        pz = (z_at + offset_of((u // 4) % 4)) % 4
-        py = (y_at + offset_of(u % 4)) % 4
-        return px * 2 + pc, pz * 4 + py
+    organs = [
+        ((x_at + dx) % 4) * 2 + (core_at + dc) % 2 for dx in (2, 3, 1, 0) for dc in (1, 0)
+    ]
+
+    def each_peer(visit):
+        def subs(i, carry):
+            z_to = (z_at + offset_of(3 - i // 4)) % 4
+            y_to = (y_at + offset_of(3 - i % 4)) % 4
+            for o in organs:
+                visit(o, z_to * 4 + y_to)
+            return carry
+
+        lax.fori_loop(0, N_SUB - 1, subs, 0)
+        for o in organs[:-1]:
+            visit(o, sub)
 
     barrier = pltpu.get_barrier_semaphore()
-
-    def greet(i, carry):
-        pl.semaphore_signal(barrier, inc=1, device_id=peer(i), device_id_type=MESH)
-        return carry
-
-    lax.fori_loop(0, N_DEV - 1, greet, 0)
+    each_peer(
+        lambda o, s: pl.semaphore_signal(barrier, inc=1, device_id=(o, s), device_id_type=MESH)
+    )
 
     loads = [pltpu.make_async_copy(mortar_hbm, m_stage, load_sem.at[0])]
     q_ref[...] = jnp.zeros(q_ref.shape, F32)
@@ -139,19 +144,17 @@
         n = ROWS[i]
         sb, rb = sends[i], recvs[i]
 
-        def go(step, carry):
-            po, ps = peer(step)
+        def send(o, s):
             pltpu.make_async_remote_copy(
-                sb.at[pl.ds((po * N_SUB + ps) * n, n)],
+                sb.at[pl.ds((o * N_SUB + s) * n, n)],
                 rb.at[pl.ds(me * n, n)],
                 send_sem.at[i],
                 recv_sem.at[i],
-                device_id=(po, ps),
+                device_id=(o, s),
                 device_id_type=MESH,
             ).start()
-            return carry
-
-        lax.fori_loop(0, N_DEV - 1, go, 0)
+
+        each_peer(send)
         pltpu.make_async_copy(
             sb.at[pl.ds(me * n, n)], rb.at[pl.ds(me * n, n)], self_sem.at[i]
         ).start()

time: 138 us -> 92.8 us (0.67)
  Pallas kernels: 131 us -> 86.5 us
    pallas_call x1, Pallas kernels: 131 us -> 86.5 us  [local(): pl.pallas_call(kernel, out_shape=jax.ShapeDtypeStruct((dirs, faces, lengt...]
where the time goes in v2:
time: 92.8 us; the launch traced here: 92.6 us
  Pallas kernels  86.5 us (93%)
  local copies, waits for them, and re-layouts  5.38 us (6%)
    pallas_call x1, Pallas kernels, local(): pl.pallas_call(kernel, out_shape=jax.ShapeDtypeStruct((dirs, faces, lengt...  86.5 us
    reshape x1, local copies, waits for them, and re-layouts, local(): warm_start.reshape(dirs, faces, length)  1.96 us
    reshape x1, local copies, waits for them, and re-layouts, local(): return result.reshape(dirs, 1, 1, faces, length)  1.86 us

profile of v2, /device:TPU:1, one launch (start us, length us, event | category | flops | bytes accessed | tf_op | source)
XLA Modules:
  0.0 92.6 jit_solution(3633666717446916109)
XLA Ops:
  0.7 1.6 %copy.25 = f32[6,1,1,5,640]{4,3,0,1,2:T(8,128)} copy(f32[6,1,1,5,640]{4,2,3,1,0:T(1,128)} %param.13) | data formatting | bytes 153600 | tf_op jit(solution)/shard_map/reshape | solution.py:634
  2.2 2.0 %copy_bitcast_fusion = (f32[16,5,640]{2,1,0:T(8,128)}, f32[16,5,640]{2,1,0:T(8,128)}) fusion(f32[16,1,1,5,640]{4,2,3,1,0:T(1,128)} %param.11, f32[16,1,1,5,640]{4,2,3,1,0:T(1,128)} %param.10), kind=kLoop, calls=%fused_computation | loop fusion | bytes 819200 | tf_op jit(solution)/shard_map/reshape | solution.py:632
  4.2 86.5 %shard_map.100 = f32[16,5,640]{2,1,0:T(8,128)} custom-call(f32[16,5,640]{2,1,0:T(8,128)} %get-tuple-element.6.rhs_hbm, f32[16,5,640]{2,1,0:T(8,128)} %get-tuple-element.5.warm_hbm, f32[5,640,640]{2,1,0:T(8,128)} %bitcast.19, f32[6,5,640]{2,1,0:T(8,128)} %bitcast.22, f32[512,640]{1,0:T(8,128)} %bitcast.21, s32[1,512]{1,0:T(1,128)} %bitcast.23, ...), custom_call_target="tpu_custom_call" | custom-call | tf_op jit(solution)/shard_map/pallas_call | solution.py:621
  90.7 1.9 %copy.18 = f32[16,1,1,5,640]{4,2,3,1,0:T(1,128)} copy(f32[16,1,1,5,640]{4,3,0,2,1:T(8,128)} %bitcast.20) | data formatting | bytes 409600 | tf_op jit(solution)/shard_map/reshape | solution.py:642

commit v3 on v2

--- a/solution.py
+++ b/solution.py
@@ -23,14 +23,6 @@
     return lax.broadcasted_iota(jnp.int32, shape, dim)
 
 
-def split3(x):
-    high = x.astype(BF16)
-    rest = x - high.astype(F32)
-    mid = rest.astype(BF16)
-    low = (rest - mid.astype(F32)).astype(BF16)
-    return high, mid, low
-
-
 def split2(x):
     high = x.astype(BF16)
     return high, (x - high.astype(F32)).astype(BF16)
@@ -42,10 +34,9 @@
 
 def mm(x, w_high, w_low):
     n = x.shape[0]
-    high, mid, low = split3(x)
-    a = dot(jnp.concatenate([high, mid, low], axis=0), w_high)
-    b = dot(jnp.concatenate([high, mid], axis=0), w_low)
-    return a[:n] + (a[n : 2 * n] + b[:n] + (a[2 * n :] + b[n:]))
+    high, low = split2(x)
+    a = dot(jnp.concatenate([high, low], axis=0), w_high)
+    return a[:n] + (a[n:] + dot(high, w_low))
 
 
 def offset_of(u):
@@ -85,9 +76,6 @@
     ym_ref,
     r_ref,
     sol_ref,
-    q_stage,
-    x_stage,
-    r_stage,
     msend,
     qsend,
     qrecv,
@@ -130,9 +118,20 @@
     loads = [pltpu.make_async_copy(mortar_hbm, m_stage, load_sem.at[0])]
     q_ref[...] = jnp.zeros(q_ref.shape, F32)
     qt_ref[...] = jnp.zeros(qt_ref.shape, F32)
-    q_loads = [pltpu.make_async_copy(coarse_hbm, q_stage, load_sem.at[1])]
-    x_loads = [pltpu.make_async_copy(warm_hbm, x_stage, load_sem.at[6])]
-    r_loads = [pltpu.make_async_copy(rhs_hbm, r_stage, load_sem.at[11])]
+    q_loads = [
+        pltpu.make_async_copy(
+            coarse_hbm.at[:, f, 0], q_ref.at[f, pl.ds(0, modes)], load_sem.at[1 + f]
+        )
+        for f in range(faces)
+    ]
+    x_loads = [
+        pltpu.make_async_copy(warm_hbm.at[:, f, 0], p_ref.at[f], load_sem.at[6 + f])
+        for f in range(faces)
+    ]
+    r_loads = [
+        pltpu.make_async_copy(rhs_hbm.at[:, f, 0], r_ref.at[f], load_sem.at[11 + f])
+        for f in range(faces)
+    ]
     g_loads = [
         pltpu.make_async_copy(inv_hbm.at[f], g_stage.at[f], load_sem.at[16 + f])
         for f in range(faces)
@@ -223,8 +222,6 @@
 
     for copy in q_loads:
         copy.wait()
-    for f in range(faces):
-        q_ref[f, :modes] = q_stage[:, f, :]
     gram = jnp.zeros((8, LANES), F32)
     for f in range(faces):
         own = q_ref[f, :8]
@@ -272,8 +269,6 @@
 
     for copy in r_loads:
         copy.wait()
-    for f in range(faces):
-        r_ref[f] = r_stage[:, f, :]
     rhs_modes = []
     for m in range(modes):
         total = r_ref[0] * q_ref[0, m : m + 1]
@@ -284,8 +279,6 @@
 
     for copy in x_loads:
         copy.wait()
-    for f in range(faces):
-        p_ref[f] = x_stage[:, f, :]
     copies = start_match(p_ref, msend.at[0], mrecv[0], ms_sem.at[0], mr_sem.at[0])
     for r in range(N_MATCH):
         qsend[r] = q_ref[face_of[r], :8]
@@ -303,26 +296,21 @@
     in_group = iota((N_DEV, LANES), 0) // N_SUB == org
     gram_row = jnp.sum(jnp.where(in_group, table, 0.0), axis=0, keepdims=True)
     for k in range(CAP):
-        column = table[:, k : k + 1].astype(jnp.int32)
-        hit = iota((N_DEV, length), 1) == column
-        wb_high[slots + k * N_DEV : slots + (k + 1) * N_DEV, :] = jnp.where(hit, -1.0, 0.0).astype(BF16)
         hit = iota((length, N_DEV), 0) == table_t[k : k + 1, :].astype(jnp.int32)
         wf_high[:, slots + k * N_DEV : slots + (k + 1) * N_DEV] = jnp.where(hit, 1.0, 0.0).astype(BF16)
 
     def row_values(x):
         n = x.shape[0]
-        high, mid, low = split3(x)
-        full = dot(jnp.concatenate([high, mid, low], axis=0), wf_high[...])
-        fine = dot(jnp.concatenate([high, mid], axis=0), wf_low[...])
-        full = full[:n] + (full[n : 2 * n] + full[2 * n :])
-        return full[:, :slots] + (fine[:n] + fine[n:]), full[:, slots:]
+        high, low = split2(x)
+        full = dot(jnp.concatenate([high, low], axis=0), wf_high[...])
+        full = full[:n] + full[n:]
+        return full[:, :slots] + dot(high, wf_low[...]), full[:, slots:]
 
     def spread_gaps(gaps):
         n = gaps.shape[0]
-        high, mid, low = split3(gaps)
-        full = dot(jnp.concatenate([high, mid, low], axis=0), wb_high[...])
-        fine = dot(jnp.concatenate([high[:, :slots], mid[:, :slots]], axis=0), wb_low[...])
-        return full[:n] + (full[n : 2 * n] + fine[:n] + (full[2 * n :] + fine[n:]))
+        high, low = split2(gaps)
+        full = dot(jnp.concatenate([high, low], axis=0), wb_high[...])
+        return full[:n] + (full[n:] + dot(high[:, :slots], wb_low[...]))
 
     def stacked(value):
         return jnp.concatenate(
@@ -347,6 +335,11 @@
     put(1, 2, jnp.broadcast_to(rhs_row, (N_DEV, LANES)))
     put(1, 3, jnp.concatenate([stacked(qa), stacked(qs)], axis=0).T)
     start_round(1)
+
+    for k in range(CAP):
+        column = table[:, k : k + 1].astype(jnp.int32)
+        hit = iota((N_DEV, length), 1) == column
+        wb_high[slots + k * N_DEV : slots + (k + 1) * N_DEV, :] = jnp.where(hit, -1.0, 0.0).astype(BF16)
 
     def gram_at(i, j):
         at = 64 + 8 * i + j
@@ -386,8 +379,31 @@
 
         lax.fori_loop(0, length // chunk, halve, 0)
 
+    def make_wide(f, extra):
+        at_round = round_of[f]
+        other = jnp.where(
+            at_round < 3,
+            org,
+            jnp.where(at_round == 3, org + 1 - 2 * (org % 2), org + 2 - 4 * ((org // 2) % 2)),
+        )
+        arrived = qrecv[at_round]
+        organ_col = iota((8, length), 0)
+        parts = []
+        for m in range(modes):
+            part = jnp.where(organ_col == org, q_ref[f, m : m + 1], 0.0) - jnp.where(
+                organ_col == other, arrived[m : m + 1], 0.0
+            )
+            if extra is not None:
+                part = part + extra[8 * m : 8 * m + 8]
+            parts.append(part)
+        parts.append(jnp.zeros((LANES - 8 * modes, length), F32))
+        high, low = split2(jnp.concatenate(parts, axis=0).T)
+        wt_high[f] = high
+        wt_low[f] = low
+
     rho = None
     c_res = None
+    coarse_rest = None
     for t in range(ITERS + 1):
         a_round = 1 + 2 * t
         for copy in copies:
@@ -403,12 +419,19 @@
             return carry
 
         lax.fori_loop(1, faces, smooth_face, 0)
+        if t == 0:
+            for copy in q_copies:
+                copy.wait()
+            for f in range(1, faces):
+                make_wide(f, None)
+        if t < ITERS:
+            coarse_part = mm(ym_ref[1], wt_high[1], wt_low[1])
+            for f in range(2, faces):
+                coarse_part = coarse_part + mm(ym_ref[f], wt_high[f], wt_low[f])
 
         wait_round(a_round)
         gaps = face_gaps(a_round, mine_a, mine_s)
         if t == 0:
-            for copy in q_copies:
-                copy.wait()
             c_row = jnp.sum(jnp.where(in_group, got(1, 2), 0.0), axis=0, keepdims=True)
             c_res = [to_column(c_row, m) for m in range(modes)]
             theirs = got(1, 3).T
@@ -432,30 +455,7 @@
             mode_gaps = jnp.concatenate(blocks, axis=0)
             both = spread_gaps(jnp.concatenate([gaps, mode_gaps], axis=0))
             contact, mode_contact = both[:dirs], both[dirs:]
-            organ_col = iota((8, length), 0)
-            for f in range(faces):
-                at_round = round_of[f]
-                other = jnp.where(
-                    at_round < 3,
-                    org,
-                    jnp.where(
-                        at_round == 3, org + 1 - 2 * (org % 2), org + 2 - 4 * ((org // 2) % 2)
-                    ),
-                )
-                arrived = qrecv[at_round]
-                parts = []
-                for m in range(modes):
-                    part = jnp.where(organ_col == org, q_ref[f, m : m + 1], 0.0) - jnp.where(
-                        organ_col == other, arrived[m : m + 1], 0.0
-                    )
-                    if f == 0:
-                        part = part + mode_contact[8 * m : 8 * m + 8]
-                    parts.append(part)
-                parts.append(jnp.zeros((LANES - 8 * modes, length), F32))
-                wide = jnp.concatenate(parts, axis=0).T
-                high, low = split2(wide)
-                wt_high[f] = high
-                wt_low[f] = low
+            make_wide(0, mode_contact)
         else:
             contact = spread_gaps(gaps)
             rho_new = to_column(jnp.sum(got(a_round, 2), axis=0, keepdims=True), 0)
@@ -493,9 +493,8 @@
         mine_a, mine_s = stacked(mine_a), stacked(mine_s)
         put(b_round, 0, mine_a.T)
         put(b_round, 1, mine_s.T)
-        coarse = mm(y_ref[0], wt_high[0], wt_low[0])
-        for f in range(1, faces):
-            coarse = coarse + mm(y_ref[f], wt_high[f], wt_low[f])
+        coarse_rest = coarse_part + beta * coarse_rest if t > 1 else coarse_part
+        coarse = coarse_rest + mm(y_ref[0], wt_high[0], wt_low[0])
         coarse = jnp.concatenate([coarse, jnp.zeros((LANES - dirs, LANES), F32)], axis=0).T
         parts = [coarse[8 * m : 8 * m + 8, :dirs] for m in range(modes)]
         parts.append(jnp.zeros((8, LANES - modes * dirs), F32))
@@ -553,11 +552,14 @@
         )
         start_round(b_round + 1)
 
-    for f in range(faces):
-        x_stage[:, f, :] = sol_ref[f]
-    write = pltpu.make_async_copy(x_stage, out_hbm, out_sem.at[0])
-    write.start()
-    write.wait()
+    writes = [
+        pltpu.make_async_copy(sol_ref.at[f], out_hbm.at[:, f, 0], out_sem.at[f])
+        for f in range(faces)
+    ]
+    for copy in writes:
+        copy.start()
+    for copy in writes:
+        copy.wait()
 
 
 def local(
@@ -598,9 +600,6 @@
     ]
     scratch += [field] * 8
     scratch += [
-        pltpu.VMEM((modes, faces, length), F32),
-        pltpu.VMEM((dirs, faces, length), F32),
-        pltpu.VMEM((dirs, faces, length), F32),
         pltpu.VMEM((N_HALO, N_MATCH, dirs, length), F32),
         pltpu.VMEM((N_MATCH, 8, length), F32),
         pltpu.VMEM((N_MATCH, 8, length), F32),
@@ -620,7 +619,7 @@
     ]
     result = pl.pallas_call(
         kernel,
-        out_shape=jax.ShapeDtypeStruct((dirs, faces, length), F32),
+        out_shape=jax.ShapeDtypeStruct((dirs, faces, 1, length), F32),
         in_specs=[any_spec] * 5 + [vmem_spec] * 3 + [smem_spec] * 2,
         out_specs=any_spec,
         scratch_shapes=scratch,
@@ -628,10 +627,10 @@
             collective_id=0, has_side_effects=True, vmem_limit_bytes=60 * 2**20
         ),
     )(
-        dual_rhs.reshape(dirs, faces, length),
-        warm_start.reshape(dirs, faces, length),
+        dual_rhs.reshape(dirs, faces, 1, length),
+        warm_start.reshape(dirs, faces, 1, length),
         inverse_blocks.reshape(faces, length, length),
-        coarse_basis.reshape(modes, faces, length),
+        coarse_basis.reshape(modes, faces, 1, length),
         mortar_rows.reshape(rows, length),
         slave_owner.reshape(1, rows),
         slave_dofs.reshape(1, rows),

time: 92.8 us -> 88.7 us (0.956)
  local copies, waits for them, and re-layouts: 5.38 us -> 1.67 us
    reshape x3 -> x0, local copies, waits for them, and re-layouts: 5.38 us -> none  [the longest x1 1.96 us: local(): warm_start.reshape(dirs, faces, length)]
    unnamed x0 -> x1, local copies, waits for them, and re-layouts: none -> 1.67 us
where the time goes in v3:
time: 88.7 us; the launch traced here: 88.5 us
  Pallas kernels  86.2 us (97%)
  local copies, waits for them, and re-layouts  1.67 us (2%)
    pallas_call x1, Pallas kernels, local(): pl.pallas_call(kernel, out_shape=jax.ShapeDtypeStruct((dirs, faces, 1, le...  86.2 us

profile of v3, /device:TPU:1, one launch (start us, length us, event | category | flops | bytes accessed | tf_op | source)
XLA Modules:
  0.0 88.5 jit_solution(12743336060670314853)
XLA Ops:
  0.7 86.2 %shard_map.100 = f32[16,5,1,640]{3,2,1,0:T(1,128)} custom-call(f32[16,5,1,640]{3,2,1,0:T(1,128)} %bitcast.17, f32[16,5,1,640]{3,2,1,0:T(1,128)} %bitcast.18, f32[5,640,640]{2,1,0:T(8,128)} %bitcast.14, f32[6,5,1,640]{3,2,1,0:T(1,128)} %bitcast.19, f32[512,640]{1,0:T(8,128)} %bitcast.15, s32[1,512]{1,0:T(1,128)} %bitcast.20, s32[1,512]{1,0:T(1,128)} %bitcast.21, ...), custom_call_target="tpu_custom_call" | custom-call | tf_op jit(solution)/shard_map/pallas_call | solution.py:620
  86.9 1.7 %copy.14 = f32[16,1,1,5,640]{4,2,3,1,0:T(1,128)} copy(f32[16,1,1,5,640]{4,2,3,1,0:T(1,128)} %bitcast.16) | data formatting | bytes 409600

commit v4 on v3

--- a/solution.py
+++ b/solution.py
@@ -83,7 +83,7 @@
 ):
     sends, recvs = rest[:N_ROUND], rest[N_ROUND : 2 * N_ROUND]
     mrecv = rest[2 * N_ROUND : 2 * N_ROUND + N_HALO]
-    (load_sem, out_sem, send_sem, recv_sem, self_sem, ms_sem, mr_sem, qs_sem, qr_sem) = rest[
+    (load_sem, out_sem, send_sem, recv_sem, self_sem, ms_sem, mr_sem, qs_sem, qr_sem, ready_sem) = rest[
         2 * N_ROUND + N_HALO :
     ]
     faces, dirs, length = p_ref.shape
@@ -111,9 +111,11 @@
             visit(o, sub)
 
     barrier = pltpu.get_barrier_semaphore()
-    each_peer(
-        lambda o, s: pl.semaphore_signal(barrier, inc=1, device_id=(o, s), device_id_type=MESH)
-    )
+    for i in range(N_SUB - 1):
+        to = ((z_at + (2, 3, 1, 0)[i // 4]) % 4) * 4 + (y_at + (2, 3, 1, 0)[i % 4]) % 4
+        pl.semaphore_signal(barrier, inc=1, device_id=(org, to), device_id_type=MESH)
+    for o in organs[:-1]:
+        pl.semaphore_signal(barrier, inc=1, device_id=(o, sub), device_id_type=MESH)
 
     loads = [pltpu.make_async_copy(mortar_hbm, m_stage, load_sem.at[0])]
     q_ref[...] = jnp.zeros(q_ref.shape, F32)
@@ -136,7 +138,7 @@
         pltpu.make_async_copy(inv_hbm.at[f], g_stage.at[f], load_sem.at[16 + f])
         for f in range(faces)
     ]
-    for copy in loads + q_loads + x_loads + r_loads + g_loads:
+    for copy in q_loads + loads + r_loads + x_loads + g_loads:
         copy.start()
 
     def start_round(i):
@@ -233,7 +235,10 @@
     keep = iota((8, LANES), 1) // 8 == iota((8, LANES), 0) + 8
     table = table + jnp.sum(jnp.where(keep, gram, 0.0), axis=0, keepdims=True)
     put(0, 0, table)
-    pl.semaphore_wait(barrier, N_DEV - 1)
+    pl.semaphore_wait(barrier, N_SUB + N_ORG - 2)
+    for o in organs[:-1]:
+        pl.semaphore_signal(ready_sem, inc=1, device_id=(o, sub), device_id_type=MESH)
+    pl.semaphore_wait(ready_sem, N_ORG - 1)
     start_round(0)
 
     for copy in loads:
@@ -243,9 +248,9 @@
     def arrange(k, carry):
         at = pl.ds(pl.multiple_of(k * N_DEV, N_DEV), N_DEV)
         for part, back, ahead in ((m_high, wb_high, wf_high), (m_low, wb_low, wf_low)):
-            block = dot(pick_ref[k], part)
-            back[at, :] = block.astype(BF16)
-            ahead[:, at] = block.T.astype(BF16)
+            block = dot(pick_ref[k], part).astype(BF16)
+            back[at, :] = block
+            ahead[:, at] = block.T
         return carry
 
     lax.fori_loop(0, CAP, arrange, 0)
@@ -465,14 +470,21 @@
         ym_ref[0] = mm(yp_ref[0], g_high[0], g_low[0])
 
         for f in range(faces):
-            made = ym_ref[f]
+            y_ref[f] = ym_ref[f] + beta * y_ref[f] if t > 1 else ym_ref[f]
+        if t < ITERS:
+            copies = start_match(
+                y_ref,
+                msend.at[2 * t + 1],
+                mrecv[2 * t + 1],
+                ms_sem.at[2 * t + 1],
+                mr_sem.at[2 * t + 1],
+            )
+        for f in range(faces):
             if t > 1:
                 w_ref[f] = yp_ref[f] + beta * w_ref[f]
-                y_ref[f] = made + beta * y_ref[f]
                 d_ref[f] = p_ref[f] + beta * d_ref[f]
             else:
                 w_ref[f] = yp_ref[f]
-                y_ref[f] = made
                 d_ref[f] = p_ref[f]
         curved = inner(w_ref, y_ref)
 
@@ -486,9 +498,6 @@
                 sol_ref[f] = sol_ref[f] + step * d_ref[f]
             break
 
-        copies = start_match(
-            y_ref, msend.at[2 * t + 1], mrecv[2 * t + 1], ms_sem.at[2 * t + 1], mr_sem.at[2 * t + 1]
-        )
         mine_a, mine_s = row_values(y_ref[0])
         mine_a, mine_s = stacked(mine_a), stacked(mine_s)
         put(b_round, 0, mine_a.T)
@@ -518,10 +527,8 @@
             step = rho / to_column(total, modes)
         for f in range(faces):
             if t > 0:
-                sol_ref[f] = sol_ref[f] + step * d_ref[f]
                 r_ref[f] = r_ref[f] - step * yp_ref[f]
             else:
-                sol_ref[f] = d_ref[f]
                 r_ref[f] = r_ref[f] - yp_ref[f]
         for m in range(modes):
             c_res[m] = c_res[m] - (step * c_image[m] if t > 0 else c_image[m])
@@ -541,6 +548,8 @@
         copies = start_match(
             p_ref, msend.at[n_halo], mrecv[n_halo], ms_sem.at[n_halo], mr_sem.at[n_halo]
         )
+        for f in range(faces):
+            sol_ref[f] = sol_ref[f] + step * d_ref[f] if t > 0 else d_ref[f]
         mine_a, mine_s = row_values(p_ref[0])
         mine_a, mine_s = stacked(mine_a), stacked(mine_s)
         put(b_round + 1, 0, mine_a.T)
@@ -616,6 +625,7 @@
         dma((N_HALO, N_MATCH)),
         dma((N_MATCH,)),
         dma((N_MATCH,)),
+        pltpu.SemaphoreType.REGULAR,
     ]
     result = pl.pallas_call(
         kernel,

time: 88.7 us -> 87.9 us (level)
  no operation moved by 1% of the time
where the time goes in v4:
time: 87.9 us; the launch traced here: 87.8 us
  Pallas kernels  85.4 us (97%)
  local copies, waits for them, and re-layouts  1.67 us (2%)
    pallas_call x1, Pallas kernels, local(): pl.pallas_call(kernel, out_shape=jax.ShapeDtypeStruct((dirs, faces, 1, le...  85.4 us

profile of v4, /device:TPU:1, one launch (start us, length us, event | category | flops | bytes accessed | tf_op | source)
XLA Modules:
  0.0 87.8 jit_solution(17583906969226987845)
XLA Ops:
  0.7 85.4 %shard_map.100 = f32[16,5,1,640]{3,2,1,0:T(1,128)} custom-call(f32[16,5,1,640]{3,2,1,0:T(1,128)} %bitcast.17, f32[16,5,1,640]{3,2,1,0:T(1,128)} %bitcast.18, f32[5,640,640]{2,1,0:T(8,128)} %bitcast.14, f32[6,5,1,640]{3,2,1,0:T(1,128)} %bitcast.19, f32[512,640]{1,0:T(8,128)} %bitcast.15, s32[1,512]{1,0:T(1,128)} %bitcast.20, s32[1,512]{1,0:T(1,128)} %bitcast.21, ...), custom_call_target="tpu_custom_call" | custom-call | tf_op jit(solution)/shard_map/pallas_call | solution.py:630
  86.1 1.7 %copy.14 = f32[16,1,1,5,640]{4,2,3,1,0:T(1,128)} copy(f32[16,1,1,5,640]{4,2,3,1,0:T(1,128)} %bitcast.16) | data formatting | bytes 409600

commit v5 on v4

--- a/solution.py
+++ b/solution.py
@@ -99,14 +99,20 @@
     ]
 
     def each_peer(visit):
-        def subs(i, carry):
-            z_to = (z_at + offset_of(3 - i // 4)) % 4
-            y_to = (y_at + offset_of(3 - i % 4)) % 4
+        def subs(i, digits):
+            z_digits, y_digits = digits
+            to = (z_at + z_digits % 4) % 4 * 4 + (y_at + y_digits % 4) % 4
             for o in organs:
-                visit(o, z_to * 4 + y_to)
-            return carry
-
-        lax.fori_loop(0, N_SUB - 1, subs, 0)
+                visit(o, to)
+            return z_digits // 4, y_digits // 4
+
+        order = sorted(
+            [(z, y) for z in range(4) for y in range(4) if z or y],
+            key=lambda at: -sum(min(d, 4 - d) for d in at),
+        )
+        z_all = sum(z * 4**i for i, (z, _) in enumerate(order))
+        y_all = sum(y * 4**i for i, (_, y) in enumerate(order))
+        lax.fori_loop(0, N_SUB - 1, subs, (jnp.int32(z_all), jnp.int32(y_all)))
         for o in organs[:-1]:
             visit(o, sub)
 
@@ -198,7 +204,9 @@
         copies = []
         for r, dev in enumerate(partners()):
             send[r] = source[face_of[r]]
-        for r, dev in enumerate(partners()):
+        devices = partners()
+        for r in (1, 0, 2, 4, 3):
+            dev = devices[r]
             copy = pltpu.make_async_remote_copy(
                 send.at[r], recv.at[r], s_sem.at[r], r_sem.at[r], device_id=dev, device_id_type=MESH
             )

time: 87.9 us -> 87.7 us (level)
  no operation moved by 1% of the time
where the time goes in v5:
time: 87.7 us; the launch traced here: 87.6 us
  Pallas kernels  85.3 us (97%)
  local copies, waits for them, and re-layouts  1.67 us (2%)
    pallas_call x1, Pallas kernels, local(): pl.pallas_call(kernel, out_shape=jax.ShapeDtypeStruct((dirs, faces, 1, le...  85.3 us

profile of v5, /device:TPU:1, one launch (start us, length us, event | category | flops | bytes accessed | tf_op | source)
XLA Modules:
  0.0 87.6 jit_solution(8595306898741618387)
XLA Ops:
  0.7 85.3 %shard_map.100 = f32[16,5,1,640]{3,2,1,0:T(1,128)} custom-call(f32[16,5,1,640]{3,2,1,0:T(1,128)} %bitcast.17, f32[16,5,1,640]{3,2,1,0:T(1,128)} %bitcast.18, f32[5,640,640]{2,1,0:T(8,128)} %bitcast.14, f32[6,5,1,640]{3,2,1,0:T(1,128)} %bitcast.19, f32[512,640]{1,0:T(8,128)} %bitcast.15, s32[1,512]{1,0:T(1,128)} %bitcast.20, s32[1,512]{1,0:T(1,128)} %bitcast.21, ...), custom_call_target="tpu_custom_call" | custom-call | tf_op jit(solution)/shard_map/pallas_call | solution.py:638
  85.9 1.7 %copy.14 = f32[16,1,1,5,640]{4,2,3,1,0:T(1,128)} copy(f32[16,1,1,5,640]{4,2,3,1,0:T(1,128)} %bitcast.16) | data formatting | bytes 409600
